TPU v7x, 32 devices: a whole 2x2x4 slice. The times are simulated.
32 devices in a mesh: gx: 4 (over y, x), gy: 2 (over core), gz: 4 (over z).
Axes of the slice: x: 2, y: 2, z: 4, core: 2. Of those that a mesh axis runs over, the one named last changes fastest.
Arguments:
- load_vector: float32 [32, 32, 2048], P(('gx', 'gy', 'gz')), may hold values from -24 to 24
- matrix_tiles: float32 [512, 7, 128, 128], P(('gx', 'gy', 'gz')), may hold values from -1 to 6, as said below
- tile_cols: int32 [512, 7], P(('gx', 'gy', 'gz')), may hold values from 0 to 15, as said below
- interior_inv: float32 [384, 128, 128], P(('gx', 'gy', 'gz')), may hold values from -0.1 to 0.3, as said below
- schur_inv: float32 [32, 512, 512], P(('gx', 'gy', 'gz')), may hold values from -0.1 to 0.3, as said below
- coarse_basis: float32 [32, 128, 2048], P(('gx', 'gy', 'gz')), may hold values from -0.125 to 0.125
- coarse_inv: float32 [32, 256, 256], P(('gx', 'gy', 'gz')), may hold values from -0.2 to 0.8, as said below
- row_map: int32 [32, 4, 128], P(('gx', 'gy', 'gz')), may hold values from 0 to 127, each once within a row
- face_link: int32 [32, 4], P(('gx', 'gy', 'gz')), may hold values from 0 to 1, as said below
- coarse_id: int32 [32, 4], P(('gx', 'gy', 'gz')), may hold values from 0 to 31, as said below
Outputs:
- solution: float32 [32, 32, 2048], P(('gx', 'gy', 'gz'))
- residual: float32 [32, 32, 2048], P(('gx', 'gy', 'gz'))
Inputs may be any that keep to these rules, and one draw needn't show every extreme that they name: `matrix_tiles`: tile 0 of each block row is its diagonal tile; each subdomain's matrix is symmetric positive definite: the tile of block row i in column block j is the transpose of the tile of block row j in column block i. `tile_cols`: tile 0 of block row i sits in column block i; tiles 1 to 6 sit in column blocks i + a, i - a, i + b, i - b, i + c, i - c modulo 16, for three distinct offsets a, b, c of that subdomain between 1 and (15) // 2; every column block holds exactly 7 tiles. `interior_inv`: each block is symmetric positive definite. `schur_inv`: symmetric positive definite. `coarse_inv`: symmetric positive definite. For partners d and e of round r, entry k of row_map[d, r] and of row_map[e, r] name the same shared unknown. `face_link`: equal for the two partners of a round. coarse_id = owner * 8 + slot, owner being a gz index within the subdomain's line of 4 devices; blocks with the same target are summed. Each subdomain sends at most 2 blocks to one owner and exactly 2 to some owner.
All inputs are finite; a program needn't handle non-finite values.
Results may differ from a plain program's by a relative error of at most 0.00018.
Values sent between devices are 32-bit elements; how exact they have to be, the bound alone decides.
No kernel may reach another device: no remote copies, remote signals or barrier semaphores. Data moves between devices by JAX's collectives and lax.ppermute only.
A program may use at most 64 MiB of HBM per device.

v0:
```python
import jax
import jax.numpy as jnp
from jax import lax
from jax.sharding import PartitionSpec as P

BS = 128
NIN = 12
NRHS = 32
CW = 32
CB = 4
OCAP = 8
ITERS = 2
NB = 16
NL = 2048
HIGH = lax.Precision.HIGHEST


def partner(value, axis, distance):
    return lax.ppermute(value, axis, [(i, i ^ 1 << distance) for i in range(lax.axis_size(axis))])


def on_device(
    load_vector,
    matrix_tiles,
    tile_cols,
    interior_inv,
    schur_inv,
    coarse_basis,
    coarse_inv,
    row_map,
    face_link,
    coarse_id,
):
    load_rows = load_vector[0]
    link_vals = face_link[0]
    face_maps = row_map[0]
    basis_rows = coarse_basis[0]
    schur_mat = schur_inv[0]
    coarse_mat = coarse_inv[0]
    block_ids = coarse_id[0]
    offset = NIN * BS
    line_size = lax.axis_size("gz")
    depth_z = line_size.bit_length() - 1
    depth_y = lax.axis_size("gy").bit_length() - 1
    swap_bits = [0, 1, depth_z, depth_z + depth_y]
    link_float = link_vals.astype(jnp.float32)
    weight = jnp.concatenate(
        [jnp.ones((offset,), jnp.float32)]
        + [jnp.broadcast_to(1.0 - 0.5 * link_float[round_no], (BS,)) for round_no in range(4)]
    )
    lane_ids = jnp.arange(BS, dtype=jnp.int32)
    onehots = [
        (face_maps[round_no][:, None] == lane_ids[None, :]).astype(jnp.float32)
        for round_no in range(4)
    ]

    def assemble(vector):
        outgoing = []
        for round_no in range(4):
            face_rows = vector[:, offset + round_no * BS : offset + (round_no + 1) * BS]
            outgoing.append(jnp.einsum("nj,kj->nk", face_rows, onehots[round_no], precision=HIGH))
        pieces = [vector[:, :offset]]
        for round_no in range(4):
            incoming = partner(outgoing[round_no], ("gx", "gy", "gz"), swap_bits[round_no])
            returned = jnp.dot(incoming, onehots[round_no], precision=HIGH)
            face_rows = vector[:, offset + round_no * BS : offset + (round_no + 1) * BS]
            pieces.append(face_rows + link_float[round_no] * returned)
        return jnp.concatenate(pieces, axis=1)

    group_rows = jnp.arange(line_size * OCAP, dtype=jnp.int32)
    dense_map = (group_rows[:, None] == block_ids[None, :]).astype(jnp.float32)

    def coarse_solve(summed):
        flat_rows = summed.reshape(OCAP * CW, NRHS)
        return jnp.dot(coarse_mat, flat_rows, precision=HIGH).reshape(OCAP, CW * NRHS)

    def coarse_part(contrib):
        summed = lax.psum_scatter(
            jnp.dot(dense_map, contrib, precision=HIGH), "gz", scatter_dimension=0, tiled=True
        )
        solved = coarse_solve(summed)
        all_solved = lax.all_gather(solved, "gz", axis=0, tiled=True)
        return jnp.einsum("ab,ac->bc", dense_map, all_solved, precision=HIGH)

    def precondition(resid):
        scaled = weight * resid
        inner_part = jnp.einsum(
            "bij,nbj->nbi", interior_inv, scaled[:, :offset].reshape(NRHS, NIN, BS), precision=HIGH
        ).reshape(NRHS, offset)
        outer_part = jnp.einsum("ij,nj->ni", schur_mat, scaled[:, offset:], precision=HIGH)
        contrib = jnp.einsum("cl,nl->cn", basis_rows, scaled, precision=HIGH).reshape(CB, CW * NRHS)
        coarse_back = coarse_part(contrib).reshape(CB * CW, NRHS)
        correction = jnp.einsum("cn,cl->nl", coarse_back, basis_rows, precision=HIGH)
        return assemble(weight * (jnp.concatenate([inner_part, outer_part], axis=1) + correction))

    def local_dot(left, right):
        return jnp.sum(weight * left * right, axis=1)

    resid = assemble(load_rows)
    solution = jnp.zeros_like(resid)
    precond_res = precondition(resid)

    def global_rz(left, right):
        return lax.psum(local_dot(left, right), ("gx", "gy", "gz"))

    direction = precond_res
    rho_now = global_rz(resid, precond_res)
    for turn_no in range(ITERS):
        picked = direction.reshape(NRHS, NB, BS)[:, tile_cols]
        product = jnp.einsum("rtij,nrtj->nri", matrix_tiles, picked, precision=HIGH).reshape(
            NRHS, NL
        )
        product_dir = assemble(product)
        curve_sum = lax.psum(local_dot(direction, product_dir), ("gx", "gy", "gz"))
        step_len = (rho_now / curve_sum)[:, None]
        solution = solution + step_len * direction
        resid = resid - step_len * product_dir
        if turn_no + 1 < ITERS:
            precond_res = precondition(resid)
            rho_next = global_rz(resid, precond_res)
            direction = precond_res + (rho_next / rho_now)[:, None] * direction
            rho_now = rho_next
    return (solution[None], resid[None])


def solution(mesh):
    in_specs = (
        P(("gx", "gy", "gz"), None, None),
        P(("gx", "gy", "gz"), None, None, None),
        P(("gx", "gy", "gz"), None),
        P(("gx", "gy", "gz"), None, None),
        P(("gx", "gy", "gz"), None, None),
        P(("gx", "gy", "gz"), None, None),
        P(("gx", "gy", "gz"), None, None),
        P(("gx", "gy", "gz"), None, None),
        P(("gx", "gy", "gz"), None),
        P(("gx", "gy", "gz"), None),
    )
    out_specs = (P(("gx", "gy", "gz"), None, None), P(("gx", "gy", "gz"), None, None))
    return jax.shard_map(
        on_device, mesh=mesh, in_specs=in_specs, out_specs=out_specs, check_vma=False
    )
```

profile of v0, /device:TPU:0, one launch (start us, length us, event | category | flops | bytes accessed | tf_op | source)
XLA Modules:
  0.0 299.2 jit_solution(18162430448153305590)
XLA Ops:
  8.1 0.9 convolution_bitcast_fusion.7
  9.0 3.1 %collective-permute-start = (f32[32,128]{0,1:T(8,128)S(1)}, f32[32,128]{0,1:T(8,128)S(1)}, u32[]{:S(2)}, u32[]{:S(2)}) collective-permute-start(f32[32,128]{0,1:T(8,128)S(1)} %convolution_bitcast_fusion.7), channel_id=1, source_target_pairs={{0,1},{1,0},{2,3},{3,2},{4,5},{5,4},{6,7},{7,6},{8,9},{9,8},{10,11... | collective-permute-start | bytes 49160 | tf_op jit(solution)/shard_map/ppermute | solution.py:19
  12.1 0.9 convolution_bitcast_fusion.6
  13.1 2.7 collective-permute-start.1
  15.7 0.9 convolution_bitcast_fusion.5
  16.8 0.9 convolution_bitcast_fusion.4
  17.7 1.6 collective-permute-start.3
  19.3 0.9 slice_dynamic-update-slice_fusion.4
  20.2 1.6 bitcast_dynamic-update-slice_fusion.2
  26.6 1.5 constant_dynamic-update-slice_fusion.4
  28.2 1.7 constant_dynamic-update-slice_fusion.3
  29.9 1.6 constant_dynamic-update-slice_fusion.2
  31.5 2.2 constant_dynamic-update-slice_fusion.1
  34.4 1.1 convolution_bitcast_fusion.11
  35.8 1.5 fusion.97
  39.1 1.3 convolution_bitcast_fusion.3
  40.5 1.0 fusion.28
  41.6 12.3 %reduce-scatter.3.cloned.1.call-done = f32[8,1024]{1,0:T(8,128)} async-done(((f32[32,1024]{1,0:T(8,128)}), f32[8,1024]{1,0:T(8,128)}) %reduce-scatter.3.cloned.1.call-update) | async-done | bytes 32784 | tf_op jit(solution)/shard_map/reduce_scatter | solution.py:78
  53.9 0.8 reshape.578
  55.3 13.4 %all_gather.6 = f32[32,1024]{1,0:T(8,128)S(1)} all-gather(f32[8,1024]{1,0:T(8,128)S(1)} %reshape.579), channel_id=1, replica_groups=mesh['gx'=4,'gy'=2,'gz'=4] {'gz'}, dimensions={0}, use_global_device_ids=true | all-gather | bytes 163840 | tf_op jit(solution)/shard_map/all_gather | solution.py:82
  71.4 1.3 collective-permute-start.5
  72.7 1.5 collective-permute-start.7
  76.1 0.9 constant_dynamic-update-slice_fusion.7
  79.5 9.9 %convolution_bitcast_fusion.1 = f32[16,4,8,128]{3,2,1,0:T(8,128)S(1)} fusion(f32[32,16,7,128]{3,0,2,1:T(8,128)S(1)} %bitcast.200, f32[16,7,128,128]{3,2,1,0:T(8,128)} %param.11), kind=kOutput, calls=%fused_computation.7 | convolution fusion | flops 704643072 | bytes 9437184 | tf_op jit(solution)/shard_map/rtij,nrtj->nri/dot_general | solution.py:110
  91.2 2.0 collective-permute-start.8
  94.0 1.6 collective-permute-start.11
  98.8 0.9 constant_dynamic-update-slice_fusion.11
  99.8 0.9 constant_dynamic-update-slice_fusion.10
  100.7 1.5 constant_dynamic-update-slice_fusion.9
  102.3 39.3 %all-reduce = (f32[32]{0:T(128)S(1)}, f32[32]{0:T(128)S(1)}) all-reduce(f32[32]{0:T(128)S(1)} %get-tuple-element.3, f32[32]{0:T(128)S(1)} %get-tuple-element.2), channel_id=1, replica_groups=mesh['gx'=4,'gy'=2,'gz'=4] {'gx','gy','gz'}, use_global_device_ids=true, to_apply=%region_2.0 | all-reduce | flops 64 | bytes 512 | tf_op jit(solution)/shard_map/psum | solution.py:104
  142.9 1.1 convolution_bitcast_fusion.10
  144.2 1.5 fusion.95
  147.6 1.3 constant_dynamic-update-slice_fusion.33
  148.9 1.3 convolution_bitcast_fusion.2
  150.3 1.0 fusion.26
  151.3 14.2 %reduce-scatter.5.cloned.1.call-done = f32[8,1024]{1,0:T(8,128)} async-done(((f32[32,1024]{1,0:T(8,128)}), f32[8,1024]{1,0:T(8,128)}) %reduce-scatter.5.cloned.1.call-update) | async-done | bytes 32784 | tf_op jit(solution)/shard_map/reduce_scatter | solution.py:78
  165.5 0.8 reshape.586
  167.0 13.3 %all_gather.7 = f32[32,1024]{1,0:T(8,128)S(1)} all-gather(f32[8,1024]{1,0:T(8,128)S(1)} %reshape.587), channel_id=1, replica_groups=mesh['gx'=4,'gy'=2,'gz'=4] {'gz'}, dimensions={0}, use_global_device_ids=true | all-gather | bytes 163840 | tf_op jit(solution)/shard_map/all_gather | solution.py:82
  182.3 1.3 collective-permute-start.13
  183.6 1.5 collective-permute-start.15
  187.0 0.9 constant_dynamic-update-slice_fusion.19
  190.5 40.7 %psum.30 = f32[32]{0:T(128)S(1)} all-reduce(f32[32]{0:T(128)S(1)} %multiply_reduce_fusion.1), channel_id=1, replica_groups=mesh['gx'=4,'gy'=2,'gz'=4] {'gx','gy','gz'}, use_global_device_ids=true, to_apply=%region_7.0 | all-reduce | flops 32 | bytes 256 | tf_op jit(solution)/shard_map/psum | solution.py:104
  232.0 9.9 %convolution_bitcast_fusion = f32[16,4,8,128]{3,2,1,0:T(8,128)S(1)} fusion(f32[32,16,7,128]{3,0,2,1:T(8,128)S(1)} %bitcast.199, f32[16,7,128,128]{3,2,1,0:T(8,128)} %param.11), kind=kOutput, calls=%fused_computation.6 | convolution fusion | flops 704643072 | bytes 9437184 | tf_op jit(solution)/shard_map/rtij,nrtj->nri/dot_general | solution.py:110
  243.2 2.1 collective-permute-start.17
  245.3 2.3 collective-permute-start.19
  248.4 0.9 constant_dynamic-update-slice_fusion.39
  251.3 40.0 %psum.31 = f32[32]{0:T(128)S(1)} all-reduce(f32[32]{0:T(128)S(1)} %multiply_reduce_fusion), channel_id=1, replica_groups=mesh['gx'=4,'gy'=2,'gz'=4] {'gx','gy','gz'}, use_global_device_ids=true, to_apply=%region_9.0 | all-reduce | flops 32 | bytes 256 | tf_op jit(solution)/shard_map/psum | solution.py:114
  291.3 1.0 multiply_subtract_fusion
  (198 shorter events, 34.4 us)
Async XLA Ops:
  7.2 27.2 %copy-start = (f32[1,128,2048]{2,1,0:T(8,128)S(1)}, f32[1,128,2048]{2,1,0:T(8,128)}, u32[]{:S(2)}) copy-start(f32[1,128,2048]{2,1,0:T(8,128)} %param.15) | copy-start | bytes 3145732
  7.2 46.7 %reduce-scatter.3.cloned.1.call-start = ((), (), s32[]{:S(2)}) async-start(), calls=%async_computation.2 | async-start | bytes 163840 | tf_op jit(solution)/shard_map/reduce_scatter | solution.py:78
  8.1 25.6 %copy-start.16 = (s32[128]{0:T(128)}, s32[128]{0:T(128)S(1)}, u32[]{:S(2)}) copy-start(s32[128]{0:T(128)S(1)} %get-tuple-element.9) | copy-start | bytes 1540
  8.1 25.6 %copy-start.20 = (s32[128]{0:T(128)}, s32[128]{0:T(128)S(1)}, u32[]{:S(2)}) copy-start(s32[128]{0:T(128)S(1)} %get-tuple-element.7) | copy-start | bytes 1540
  8.1 25.6 %copy-start.23 = (s32[128]{0:T(128)}, s32[128]{0:T(128)S(1)}, u32[]{:S(2)}) copy-start(s32[128]{0:T(128)S(1)} %get-tuple-element.8) | copy-start | bytes 1540
  9.0 17.6 %collective-permute-start = (f32[32,128]{0,1:T(8,128)S(1)}, f32[32,128]{0,1:T(8,128)S(1)}, u32[]{:S(2)}, u32[]{:S(2)}) collective-permute-start(f32[32,128]{0,1:T(8,128)S(1)} %convolution_bitcast_fusion.7), channel_id=1, source_target_pairs={{0,1},{1,0},{2,3},{3,2},{4,5},{5,4},{6,7},{7,6},{8,9},{9,8},{10,11... | collective-permute-start | bytes 49160 | tf_op jit(solution)/shard_map/ppermute | solution.py:19
  13.1 15.1 %collective-permute-start.1 = (f32[32,128]{0,1:T(8,128)S(1)}, f32[32,128]{0,1:T(8,128)S(1)}, u32[]{:S(2)}, u32[]{:S(2)}) collective-permute-start(f32[32,128]{0,1:T(8,128)S(1)} %convolution_bitcast_fusion.6), channel_id=1, source_target_pairs={{0,2},{1,3},{2,0},{3,1},{4,6},{5,7},{6,4},{7,5},{8,10},{9,11},{10,... | collective-permute-start | bytes 49160 | tf_op jit(solution)/shard_map/ppermute | solution.py:19
  16.7 13.2 %collective-permute-start.2 = (f32[32,128]{0,1:T(8,128)S(1)}, f32[32,128]{0,1:T(8,128)S(1)}, u32[]{:S(2)}, u32[]{:S(2)}) collective-permute-start(f32[32,128]{0,1:T(8,128)S(1)} %convolution_bitcast_fusion.5), channel_id=1, source_target_pairs={{0,4},{1,5},{2,6},{3,7},{4,0},{5,1},{6,2},{7,3},{8,12},{9,13},{10,... | collective-permute-start | bytes 49160 | tf_op jit(solution)/shard_map/ppermute | solution.py:19
  17.7 21.4 %copy-start.7 = (f32[12,128,128]{2,1,0:T(8,128)S(1)}, f32[12,128,128]{2,1,0:T(8,128)}, u32[]{:S(2)}) copy-start(f32[12,128,128]{2,1,0:T(8,128)} %param.13) | copy-start | bytes 2359300
  17.7 13.7 %collective-permute-start.3 = (f32[32,128]{0,1:T(8,128)S(1)}, f32[32,128]{0,1:T(8,128)S(1)}, u32[]{:S(2)}, u32[]{:S(2)}) collective-permute-start(f32[32,128]{0,1:T(8,128)S(1)} %convolution_bitcast_fusion.4), channel_id=1, source_target_pairs={{0,8},{1,9},{2,10},{3,11},{4,12},{5,13},{6,14},{7,15},{8,0},{9,1},... | collective-permute-start | bytes 49160 | tf_op jit(solution)/shard_map/ppermute | solution.py:19
  35.6 19.2 %copy-start.9 = (f32[1,256,256]{2,1,0:T(8,128)S(1)}, f32[1,256,256]{2,1,0:T(8,128)}, u32[]{:S(2)}) copy-start(f32[1,256,256]{2,1,0:T(8,128)} %param.16) | copy-start | bytes 786436
  37.3 128.2 %reduce-scatter.5.cloned.1.call-start = ((), (), s32[]{:S(2)}) async-start(), calls=%async_computation.3 | async-start | bytes 163840 | tf_op jit(solution)/shard_map/reduce_scatter | solution.py:78
  39.1 29.5 %copy-start.26 = (s32[1,4]{1,0:T(1,128)S(1)}, s32[1,4]{1,0:T(1,128)}, u32[]{:S(2)}) copy-start(s32[1,4]{1,0:T(1,128)} %param.19) | copy-start | bytes 52
  41.6 28.1 %copy-start.24 = (s32[128]{0:T(128)S(1)}, s32[128]{0:T(128)}, u32[]{:S(2)}) copy-start(s32[128]{0:T(128)} %copy-done.23) | copy-start | bytes 1540
  41.6 28.3 %copy-start.21 = (s32[128]{0:T(128)S(1)}, s32[128]{0:T(128)}, u32[]{:S(2)}) copy-start(s32[128]{0:T(128)} %copy-done.20) | copy-start | bytes 1540
  41.6 28.6 %copy-start.17 = (s32[128]{0:T(128)S(1)}, s32[128]{0:T(128)}, u32[]{:S(2)}) copy-start(s32[128]{0:T(128)} %copy-done.16) | copy-start | bytes 1540
  71.2 3.7 %collective-permute-start.4 = (f32[32,128]{1,0:T(8,128)S(1)}, f32[32,128]{1,0:T(8,128)S(1)}, u32[]{:S(2)}, u32[]{:S(2)}) collective-permute-start(f32[32,128]{1,0:T(8,128)S(1)} %fusion.53), channel_id=1, source_target_pairs={{0,1},{1,0},{2,3},{3,2},{4,5},{5,4},{6,7},{7,6},{8,9},{9,8},{10,11... | collective-permute-start | bytes 49160 | tf_op jit(solution)/shard_map/ppermute | solution.py:19
  71.4 4.7 %collective-permute-start.5 = (f32[32,128]{1,0:T(8,128)S(1)}, f32[32,128]{1,0:T(8,128)S(1)}, u32[]{:S(2)}, u32[]{:S(2)}) collective-permute-start(f32[32,128]{1,0:T(8,128)S(1)} %fusion.49), channel_id=1, source_target_pairs={{0,2},{1,3},{2,0},{3,1},{4,6},{5,7},{6,4},{7,5},{8,10},{9,11},{10,... | collective-permute-start | bytes 49160 | tf_op jit(solution)/shard_map/ppermute | solution.py:19
  72.7 4.3 %collective-permute-start.6 = (f32[32,128]{1,0:T(8,128)S(1)}, f32[32,128]{1,0:T(8,128)S(1)}, u32[]{:S(2)}, u32[]{:S(2)}) collective-permute-start(f32[32,128]{1,0:T(8,128)S(1)} %fusion.45), channel_id=1, source_target_pairs={{0,4},{1,5},{2,6},{3,7},{4,0},{5,1},{6,2},{7,3},{8,12},{9,13},{10,... | collective-permute-start | bytes 49160 | tf_op jit(solution)/shard_map/ppermute | solution.py:19
  72.7 5.2 %collective-permute-start.7 = (f32[32,128]{1,0:T(8,128)S(1)}, f32[32,128]{1,0:T(8,128)S(1)}, u32[]{:S(2)}, u32[]{:S(2)}) collective-permute-start(f32[32,128]{1,0:T(8,128)S(1)} %fusion.41), channel_id=1, source_target_pairs={{0,8},{1,9},{2,10},{3,11},{4,12},{5,13},{6,14},{7,15},{8,0},{9,1},... | collective-permute-start | bytes 49160 | tf_op jit(solution)/shard_map/ppermute | solution.py:19
  79.5 17.9 %copy-start.15 = (f32[32,128]{1,0:T(8,128)S(1)}, f32[32,128]{1,0:T(8,128)}, u32[]{:S(2)}) copy-start(f32[32,128]{1,0:T(8,128)} %get-tuple-element.23) | copy-start | bytes 49156
  89.4 12.8 %copy-start.6 = (f32[32,2048]{1,0:T(8,128)S(1)}, f32[32,2048]{1,0:T(8,128)}, u32[]{:S(2)}) copy-start(f32[32,2048]{1,0:T(8,128)} %copy-done.5) | copy-start | bytes 786436
  91.2 6.8 %collective-permute-start.8 = (f32[32,128]{1,0:T(8,128)S(1)}, f32[32,128]{1,0:T(8,128)S(1)}, u32[]{:S(2)}, u32[]{:S(2)}) collective-permute-start(f32[32,128]{1,0:T(8,128)S(1)} %fusion.52), channel_id=1, source_target_pairs={{0,1},{1,0},{2,3},{3,2},{4,5},{5,4},{6,7},{7,6},{8,9},{9,8},{10,11... | collective-permute-start | bytes 49160 | tf_op jit(solution)/shard_map/ppermute | solution.py:19
  93.2 5.6 %collective-permute-start.9 = (f32[32,128]{1,0:T(8,128)S(1)}, f32[32,128]{1,0:T(8,128)S(1)}, u32[]{:S(2)}, u32[]{:S(2)}) collective-permute-start(f32[32,128]{1,0:T(8,128)S(1)} %fusion.48), channel_id=1, source_target_pairs={{0,2},{1,3},{2,0},{3,1},{4,6},{5,7},{6,4},{7,5},{8,10},{9,11},{10,... | collective-permute-start | bytes 49160 | tf_op jit(solution)/shard_map/ppermute | solution.py:19
  94.0 5.7 %collective-permute-start.10 = (f32[32,128]{1,0:T(8,128)S(1)}, f32[32,128]{1,0:T(8,128)S(1)}, u32[]{:S(2)}, u32[]{:S(2)}) collective-permute-start(f32[32,128]{1,0:T(8,128)S(1)} %fusion.44), channel_id=1, source_target_pairs={{0,4},{1,5},{2,6},{3,7},{4,0},{5,1},{6,2},{7,3},{8,12},{9,13},{10,... | collective-permute-start | bytes 49160 | tf_op jit(solution)/shard_map/ppermute | solution.py:19
  94.0 6.7 %collective-permute-start.11 = (f32[32,128]{1,0:T(8,128)S(1)}, f32[32,128]{1,0:T(8,128)S(1)}, u32[]{:S(2)}, u32[]{:S(2)}) collective-permute-start(f32[32,128]{1,0:T(8,128)S(1)} %fusion.40), channel_id=1, source_target_pairs={{0,8},{1,9},{2,10},{3,11},{4,12},{5,13},{6,14},{7,15},{8,0},{9,1},... | collective-permute-start | bytes 49160 | tf_op jit(solution)/shard_map/ppermute | solution.py:19
  99.8 49.1 %copy-start.8 = (f32[12,128,128]{2,1,0:T(8,128)S(1)}, f32[12,128,128]{2,1,0:T(8,128)}, u32[]{:S(2)}) copy-start(f32[12,128,128]{2,1,0:T(8,128)} %param.13) | copy-start | bytes 2359300
  148.9 31.4 %copy-start.27 = (s32[1,4]{1,0:T(1,128)S(1)}, s32[1,4]{1,0:T(1,128)}, u32[]{:S(2)}) copy-start(s32[1,4]{1,0:T(1,128)} %param.19) | copy-start | bytes 52
  150.2 16.2 %copy-start.10 = (f32[1,256,256]{2,1,0:T(8,128)S(1)}, f32[1,256,256]{2,1,0:T(8,128)}, u32[]{:S(2)}) copy-start(f32[1,256,256]{2,1,0:T(8,128)} %param.16) | copy-start | bytes 786436
  151.3 30.0 %copy-start.25 = (s32[128]{0:T(128)S(1)}, s32[128]{0:T(128)}, u32[]{:S(2)}) copy-start(s32[128]{0:T(128)} %copy-done.23) | copy-start | bytes 1540
  151.3 30.2 %copy-start.22 = (s32[128]{0:T(128)S(1)}, s32[128]{0:T(128)}, u32[]{:S(2)}) copy-start(s32[128]{0:T(128)} %copy-done.20) | copy-start | bytes 1540
  151.3 30.5 %copy-start.19 = (s32[128]{0:T(128)S(1)}, s32[128]{0:T(128)}, u32[]{:S(2)}) copy-start(s32[128]{0:T(128)} %copy-done.16) | copy-start | bytes 1540
  180.3 50.8 %copy-start.31 = (f32[32]{0:T(128)S(1)}, f32[32]{0:T(128)}, u32[]{:S(2)}) copy-start(f32[32]{0:T(128)} %copy-done.30) | copy-start | bytes 388
  182.0 3.8 %collective-permute-start.12 = (f32[32,128]{1,0:T(8,128)S(1)}, f32[32,128]{1,0:T(8,128)S(1)}, u32[]{:S(2)}, u32[]{:S(2)}) collective-permute-start(f32[32,128]{1,0:T(8,128)S(1)} %fusion.51), channel_id=1, source_target_pairs={{0,1},{1,0},{2,3},{3,2},{4,5},{5,4},{6,7},{7,6},{8,9},{9,8},{10,11... | collective-permute-start | bytes 49160 | tf_op jit(solution)/shard_map/ppermute | solution.py:19
  182.3 4.7 %collective-permute-start.13 = (f32[32,128]{1,0:T(8,128)S(1)}, f32[32,128]{1,0:T(8,128)S(1)}, u32[]{:S(2)}, u32[]{:S(2)}) collective-permute-start(f32[32,128]{1,0:T(8,128)S(1)} %fusion.47), channel_id=1, source_target_pairs={{0,2},{1,3},{2,0},{3,1},{4,6},{5,7},{6,4},{7,5},{8,10},{9,11},{10,... | collective-permute-start | bytes 49160 | tf_op jit(solution)/shard_map/ppermute | solution.py:19
  183.6 4.3 %collective-permute-start.14 = (f32[32,128]{1,0:T(8,128)S(1)}, f32[32,128]{1,0:T(8,128)S(1)}, u32[]{:S(2)}, u32[]{:S(2)}) collective-permute-start(f32[32,128]{1,0:T(8,128)S(1)} %fusion.43), channel_id=1, source_target_pairs={{0,4},{1,5},{2,6},{3,7},{4,0},{5,1},{6,2},{7,3},{8,12},{9,13},{10,... | collective-permute-start | bytes 49160 | tf_op jit(solution)/shard_map/ppermute | solution.py:19
  183.6 5.2 %collective-permute-start.15 = (f32[32,128]{1,0:T(8,128)S(1)}, f32[32,128]{1,0:T(8,128)S(1)}, u32[]{:S(2)}, u32[]{:S(2)}) collective-permute-start(f32[32,128]{1,0:T(8,128)S(1)} %fusion.39), channel_id=1, source_target_pairs={{0,8},{1,9},{2,10},{3,11},{4,12},{5,13},{6,14},{7,15},{8,0},{9,1},... | collective-permute-start | bytes 49160 | tf_op jit(solution)/shard_map/ppermute | solution.py:19
  189.6 41.5 %copy-start.3 = (f32[32,2048]{1,0:T(8,128)}, f32[32,2048]{1,0:T(8,128)S(1)}, u32[]{:S(2)}) copy-start(f32[32,2048]{1,0:T(8,128)S(1)} %get-tuple-element.46) | copy-start | bytes 786436
  232.0 15.5 %copy-start.14 = (f32[1,32,2048]{2,1,0:T(8,128)S(1)}, f32[1,32,2048]{2,1,0:T(8,128)}, u32[]{:S(2)}) copy-start(f32[1,32,2048]{2,1,0:T(8,128)} %bitcast_dynamic-update-slice_fusion.3) | copy-start | bytes 786436
  242.0 49.3 %copy-start.33 = (f32[32]{0:T(128)S(1)}, f32[32]{0:T(128)}, u32[]{:S(2)}) copy-start(f32[32]{0:T(128)} %copy-done.32) | copy-start | bytes 388
  242.0 49.3 %copy-start.11 = (f32[1,32,2048]{2,1,0:T(8,128)S(1)}, f32[1,32,2048]{2,1,0:T(8,128)}, u32[]{:S(2)}) copy-start(f32[1,32,2048]{2,1,0:T(8,128)} %constant_dynamic-update-slice_fusion.33) | copy-start | bytes 786436
  242.0 49.3 %copy-start.12 = (f32[1,32,2048]{2,1,0:T(8,128)S(1)}, f32[1,32,2048]{2,1,0:T(8,128)}, u32[]{:S(2)}) copy-start(f32[1,32,2048]{2,1,0:T(8,128)} %get-tuple-element.57) | copy-start | bytes 786436
  242.0 49.3 %copy-start.13 = (f32[1,32,2048]{2,1,0:T(8,128)S(1)}, f32[1,32,2048]{2,1,0:T(8,128)}, u32[]{:S(2)}) copy-start(f32[1,32,2048]{2,1,0:T(8,128)} %get-tuple-element.56) | copy-start | bytes 786436
  242.0 49.3 %copy-start.29 = (f32[32]{0:T(128)S(1)}, f32[32]{0:T(128)}, u32[]{:S(2)}) copy-start(f32[32]{0:T(128)} %copy-done.28) | copy-start | bytes 388
  243.1 4.5 %collective-permute-start.16 = (f32[32,128]{1,0:T(8,128)S(1)}, f32[32,128]{1,0:T(8,128)S(1)}, u32[]{:S(2)}, u32[]{:S(2)}) collective-permute-start(f32[32,128]{1,0:T(8,128)S(1)} %fusion.50), channel_id=1, source_target_pairs={{0,1},{1,0},{2,3},{3,2},{4,5},{5,4},{6,7},{7,6},{8,9},{9,8},{10,11... | collective-permute-start | bytes 49160 | tf_op jit(solution)/shard_map/ppermute | solution.py:19
  243.2 5.2 %collective-permute-start.17 = (f32[32,128]{1,0:T(8,128)S(1)}, f32[32,128]{1,0:T(8,128)S(1)}, u32[]{:S(2)}, u32[]{:S(2)}) collective-permute-start(f32[32,128]{1,0:T(8,128)S(1)} %fusion.46), channel_id=1, source_target_pairs={{0,2},{1,3},{2,0},{3,1},{4,6},{5,7},{6,4},{7,5},{8,10},{9,11},{10,... | collective-permute-start | bytes 49160 | tf_op jit(solution)/shard_map/ppermute | solution.py:19
  245.3 4.0 %collective-permute-start.18 = (f32[32,128]{1,0:T(8,128)S(1)}, f32[32,128]{1,0:T(8,128)S(1)}, u32[]{:S(2)}, u32[]{:S(2)}) collective-permute-start(f32[32,128]{1,0:T(8,128)S(1)} %fusion.42), channel_id=1, source_target_pairs={{0,4},{1,5},{2,6},{3,7},{4,0},{5,1},{6,2},{7,3},{8,12},{9,13},{10,... | collective-permute-start | bytes 49160 | tf_op jit(solution)/shard_map/ppermute | solution.py:19
  245.3 4.9 %collective-permute-start.19 = (f32[32,128]{1,0:T(8,128)S(1)}, f32[32,128]{1,0:T(8,128)S(1)}, u32[]{:S(2)}, u32[]{:S(2)}) collective-permute-start(f32[32,128]{1,0:T(8,128)S(1)} %fusion.38), channel_id=1, source_target_pairs={{0,8},{1,9},{2,10},{3,11},{4,12},{5,13},{6,14},{7,15},{8,0},{9,1},... | collective-permute-start | bytes 49160 | tf_op jit(solution)/shard_map/ppermute | solution.py:19
  (8 other events, 35.6 us)
Sparse Core Ops, SparseCore 0:
  37.4 16.4 reduce-scatter.2
  145.9 19.6 reduce-scatter.4
where the time goes:
time: 300 us; the launch traced here: 299 us
  blocking collectives  147 us (49%)
  matrix products  60.6 us (20%)
  waiting for transfers between devices  28.8 us (10%)
  starting transfers between devices  22 us (7%)
  local copies, waits for them, and re-layouts  20.4 us (7%)
  between operations  17.6 us (6%)
  other arithmetic  3.1 us (1%)
    psum x2, blocking collectives, global_rz(): return lax.psum(local_dot(left, right), ('gx', 'gy', 'gz'))  80 us
    psum x1, blocking collectives, on_device(): curve_sum = lax.psum(local_dot(direction, product_dir), ('gx', 'gy', 'gz'))  40 us
    all_gather x2, blocking collectives, coarse_part(): all_solved = lax.all_gather(solved, 'gz', axis=0, tiled=True)  26.7 us
    reduce_scatter x2, waiting for transfers between devices, coarse_part(): lax.psum_scatter(jnp.dot(dense_map, contrib, precision=HIGH), 'gz', scatt...  26.5 us
    ppermute x20, starting transfers between devices, partner(): lax.ppermute(value, axis, [(i, i ^ 1 << distance) for i in range(lax.axis...  21.9 us
    dot_general x20, matrix products, assemble(): returned = jnp.dot(incoming, onehots[round_no], precision=HIGH)  21 us
    dot_general x2, matrix products, on_device(): jnp.einsum('rtij,nrtj->nri', matrix_tiles, picked, precision=HIGH)  19.8 us
    unnamed x97, local copies, waits for them, and re-layouts  12.5 us
  transfers between devices with their start and end apart: 22, of which 6 were waited for; matrix products, arithmetic and copies ran while one was open for 12% of the time, Pallas kernels for 0%

commit v1 on v0

--- a/solution.py
+++ b/solution.py
@@ -79,7 +79,14 @@
             jnp.dot(dense_map, contrib, precision=HIGH), "gz", scatter_dimension=0, tiled=True
         )
         solved = coarse_solve(summed)
-        all_solved = lax.all_gather(solved, "gz", axis=0, tiled=True)
+        ring = [solved]
+        for hop in range(3):
+            ring.append(lax.ppermute(ring[-1], "gz", [(dev, (dev + 1) % 4) for dev in range(4)]))
+        all_solved = jnp.roll(
+            jnp.concatenate(ring[::-1], axis=0),
+            (lax.axis_index("gz") + 1) * ring[0].shape[0],
+            axis=0,
+        )
         return jnp.einsum("ab,ac->bc", dense_map, all_solved, precision=HIGH)
 
     def precondition(resid):

time: 300 us -> 311 us (1.037)
  waiting for transfers between devices: 28.8 us -> 65.8 us
  blocking collectives: 147 us -> 118 us
    ppermute x0 -> x6, waiting for transfers between devices: none -> 29.7 us  [coarse_part(): lax.ppermute(ring[-1], 'gz', [(dev, (dev + 1) % 4) for dev in range(4)])]
    all_gather x2 -> x0, blocking collectives: 26.7 us -> none  [coarse_part(): all_solved = lax.all_gather(solved, 'gz', axis=0, tiled=True)]
    reduce_scatter x2, waiting for transfers between devices: 26.5 us -> 31.9 us  [coarse_part(): lax.psum_scatter(jnp.dot(dense_map, contrib, precision=HIGH), 'gz', scatt...]
    unnamed x97 -> x89, local copies, waits for them, and re-layouts: 12.5 us -> 14.5 us
  transfers between devices with their start and end apart: 22 -> 28, of which waited for: 6 -> 12; matrix products, arithmetic and copies ran while one was open for 12% -> 12% of each run, Pallas kernels for 0% -> 0%
where the time goes in v1:
time: 311 us; the launch traced here: 310 us
  blocking collectives  118 us (38%)
  waiting for transfers between devices  65.8 us (21%)
  matrix products  62.6 us (20%)
  local copies, waits for them, and re-layouts  22.3 us (7%)
  starting transfers between devices  19.7 us (6%)
  between operations  17.6 us (6%)
  other arithmetic  4.06 us (1%)
    psum x2, blocking collectives, global_rz(): return lax.psum(local_dot(left, right), ('gx', 'gy', 'gz'))  80.1 us
    psum x1, blocking collectives, on_device(): curve_sum = lax.psum(local_dot(direction, product_dir), ('gx', 'gy', 'gz'))  38 us
    reduce_scatter x2, waiting for transfers between devices, coarse_part(): lax.psum_scatter(jnp.dot(dense_map, contrib, precision=HIGH), 'gz', scatt...  31.9 us
    ppermute x6, waiting for transfers between devices, coarse_part(): lax.ppermute(ring[-1], 'gz', [(dev, (dev + 1) % 4) for dev in range(4)])  29.7 us
    dot_general x20, matrix products, assemble(): returned = jnp.dot(incoming, onehots[round_no], precision=HIGH)  21.1 us
    dot_general x2, matrix products, on_device(): jnp.einsum('rtij,nrtj->nri', matrix_tiles, picked, precision=HIGH)  19.8 us
    ppermute x20, starting transfers between devices, partner(): lax.ppermute(value, axis, [(i, i ^ 1 << distance) for i in range(lax.axis...  19.5 us
    unnamed x89, local copies, waits for them, and re-layouts  14.5 us
  transfers between devices with their start and end apart: 28, of which 12 were waited for; matrix products, arithmetic and copies ran while one was open for 12% of the time, Pallas kernels for 0%

profile of v1, /device:TPU:0, one launch (start us, length us, event | category | flops | bytes accessed | tf_op | source)
XLA Modules:
  0.0 310.1 jit_solution(13912677524515277889)
XLA Ops:
  8.1 0.9 convolution_bitcast_fusion.7
  9.0 3.1 collective-permute-start
  12.1 0.9 convolution_bitcast_fusion.6
  13.1 2.7 collective-permute-start.1
  15.7 0.9 convolution_bitcast_fusion.5
  16.8 0.9 convolution_bitcast_fusion.4
  17.7 1.6 collective-permute-start.3
  19.3 0.9 slice_dynamic-update-slice_fusion.4
  20.2 1.7 bitcast_dynamic-update-slice_fusion.2
  26.7 1.7 constant_dynamic-update-slice_fusion.4
  28.4 1.5 constant_dynamic-update-slice_fusion.3
  30.0 1.5 constant_dynamic-update-slice_fusion.2
  31.5 2.3 constant_dynamic-update-slice_fusion.1
  33.8 1.1 convolution_bitcast_fusion.11
  35.2 1.5 fusion.115
  37.3 1.0 fusion.28
  38.4 14.9 %reduce-scatter.3.cloned.1.call-done = f32[8,1024]{1,0:T(8,128)} async-done(((f32[32,1024]{1,0:T(8,128)}), f32[8,1024]{1,0:T(8,128)}) %reduce-scatter.3.cloned.1.call-update) | async-done | bytes 32784 | tf_op jit(solution)/shard_map/reduce_scatter | solution.py:78
  54.2 1.3 convolution_bitcast_fusion.9
  56.4 5.1 %collective-permute-done.4 = f32[8,1024]{1,0:T(8,128)S(1)} collective-permute-done((f32[8,1024]{1,0:T(8,128)S(1)}, f32[8,1024]{1,0:T(8,128)S(1)}, u32[]{:S(2)}, u32[]{:S(2)}) %collective-permute-start.4) | collective-permute-done | bytes 32800 | tf_op jit(solution)/shard_map/ppermute | solution.py:84
  62.1 5.4 %collective-permute-done.5 = f32[8,1024]{1,0:T(8,128)S(1)} collective-permute-done((f32[8,1024]{1,0:T(8,128)S(1)}, f32[8,1024]{1,0:T(8,128)S(1)}, u32[]{:S(2)}, u32[]{:S(2)}) %collective-permute-start.5) | collective-permute-done | bytes 32800 | tf_op jit(solution)/shard_map/ppermute | solution.py:84
  67.5 1.3 convolution_bitcast_fusion.3
  68.9 4.3 %collective-permute-done.6 = f32[8,1024]{1,0:T(8,128)S(1)} collective-permute-done((f32[8,1024]{1,0:T(8,128)S(1)}, f32[8,1024]{1,0:T(8,128)S(1)}, u32[]{:S(2)}, u32[]{:S(2)}) %collective-permute-start.6) | collective-permute-done | bytes 32800 | tf_op jit(solution)/shard_map/ppermute | solution.py:84
  76.3 1.5 collective-permute-start.10
  77.8 1.7 collective-permute-done.7
  82.2 0.9 constant_dynamic-update-slice_fusion.5
  84.0 9.9 %convolution_bitcast_fusion.1 = f32[16,4,8,128]{3,2,1,0:T(8,128)S(1)} fusion(f32[32,16,7,128]{3,0,2,1:T(8,128)S(1)} %bitcast.198, f32[16,7,128,128]{3,2,1,0:T(8,128)} %param.13), kind=kOutput, calls=%fused_computation.7 | convolution fusion | flops 704643072 | bytes 9437184 | tf_op jit(solution)/shard_map/rtij,nrtj->nri/dot_general | solution.py:117
  95.7 2.0 collective-permute-start.11
  98.5 1.2 collective-permute-start.14
  103.0 1.5 constant_dynamic-update-slice_fusion.11
  106.4 39.6 %all-reduce = (f32[32]{0:T(128)S(1)}, f32[32]{0:T(128)S(1)}) all-reduce(f32[32]{0:T(128)S(1)} %get-tuple-element.4, f32[32]{0:T(128)S(1)} %get-tuple-element.3), channel_id=1, replica_groups=mesh['gx'=4,'gy'=2,'gz'=4] {'gx','gy','gz'}, use_global_device_ids=true, to_apply=%region_2.4 | all-reduce | flops 64 | bytes 512 | tf_op jit(solution)/shard_map/psum | solution.py:111
  147.3 1.1 convolution_bitcast_fusion.10
  148.6 1.5 fusion.114
  150.7 1.3 constant_dynamic-update-slice_fusion.35
  152.1 1.0 fusion.26
  153.1 17.0 %reduce-scatter.5.cloned.1.call-done = f32[8,1024]{1,0:T(8,128)} async-done(((f32[32,1024]{1,0:T(8,128)}), f32[8,1024]{1,0:T(8,128)}) %reduce-scatter.5.cloned.1.call-update) | async-done | bytes 32784 | tf_op jit(solution)/shard_map/reduce_scatter | solution.py:78
  171.0 1.3 convolution_bitcast_fusion.8
  173.2 5.1 %collective-permute-done.15 = f32[8,1024]{1,0:T(8,128)S(1)} collective-permute-done((f32[8,1024]{1,0:T(8,128)S(1)}, f32[8,1024]{1,0:T(8,128)S(1)}, u32[]{:S(2)}, u32[]{:S(2)}) %collective-permute-start.15) | collective-permute-done | bytes 32800 | tf_op jit(solution)/shard_map/ppermute | solution.py:84
  178.9 5.4 %collective-permute-done.16 = f32[8,1024]{1,0:T(8,128)S(1)} collective-permute-done((f32[8,1024]{1,0:T(8,128)S(1)}, f32[8,1024]{1,0:T(8,128)S(1)}, u32[]{:S(2)}, u32[]{:S(2)}) %collective-permute-start.16) | collective-permute-done | bytes 32800 | tf_op jit(solution)/shard_map/ppermute | solution.py:84
  184.3 1.3 convolution_bitcast_fusion.2
  185.7 4.3 %collective-permute-done.17 = f32[8,1024]{1,0:T(8,128)S(1)} collective-permute-done((f32[8,1024]{1,0:T(8,128)S(1)}, f32[8,1024]{1,0:T(8,128)S(1)}, u32[]{:S(2)}, u32[]{:S(2)}) %collective-permute-start.17) | collective-permute-done | bytes 32800 | tf_op jit(solution)/shard_map/ppermute | solution.py:84
  192.4 1.5 collective-permute-start.21
  193.9 1.7 collective-permute-done.18
  200.2 40.5 %psum.30 = f32[32]{0:T(128)S(1)} all-reduce(f32[32]{0:T(128)S(1)} %multiply_reduce_fusion.1), channel_id=1, replica_groups=mesh['gx'=4,'gy'=2,'gz'=4] {'gx','gy','gz'}, use_global_device_ids=true, to_apply=%region_7.9 | all-reduce | flops 32 | bytes 256 | tf_op jit(solution)/shard_map/psum | solution.py:111
  241.6 9.9 %convolution_bitcast_fusion = f32[16,4,8,128]{3,2,1,0:T(8,128)S(1)} fusion(f32[32,16,7,128]{3,0,2,1:T(8,128)S(1)} %bitcast.197, f32[16,7,128,128]{3,2,1,0:T(8,128)} %param.13), kind=kOutput, calls=%fused_computation.6 | convolution fusion | flops 704643072 | bytes 9437184 | tf_op jit(solution)/shard_map/rtij,nrtj->nri/dot_general | solution.py:117
  252.7 2.2 collective-permute-start.23
  254.8 2.3 collective-permute-start.25
  263.3 38.0 %psum.31 = f32[32]{0:T(128)S(1)} all-reduce(f32[32]{0:T(128)S(1)} %multiply_reduce_fusion), channel_id=1, replica_groups=mesh['gx'=4,'gy'=2,'gz'=4] {'gx','gy','gz'}, use_global_device_ids=true, to_apply=%region_9.11 | all-reduce | flops 32 | bytes 256 | tf_op jit(solution)/shard_map/psum | solution.py:121
  301.4 1.9 multiply_subtract_fusion
  (200 shorter events, 40.0 us)
Async XLA Ops:
  7.2 26.7 %copy-start = (f32[1,128,2048]{2,1,0:T(8,128)S(1)}, f32[1,128,2048]{2,1,0:T(8,128)}, u32[]{:S(2)}) copy-start(f32[1,128,2048]{2,1,0:T(8,128)} %param.17) | copy-start | bytes 3145732
  7.2 46.1 %reduce-scatter.3.cloned.1.call-start = ((), (), s32[]{:S(2)}) async-start(), calls=%async_computation.2 | async-start | bytes 163840 | tf_op jit(solution)/shard_map/reduce_scatter | solution.py:78
  8.1 25.7 %copy-start.13 = (s32[128]{0:T(128)}, s32[128]{0:T(128)S(1)}, u32[]{:S(2)}) copy-start(s32[128]{0:T(128)S(1)} %get-tuple-element.10) | copy-start | bytes 1540
  8.1 25.7 %copy-start.16 = (s32[128]{0:T(128)}, s32[128]{0:T(128)S(1)}, u32[]{:S(2)}) copy-start(s32[128]{0:T(128)S(1)} %get-tuple-element.8) | copy-start | bytes 1540
  8.1 25.7 %copy-start.19 = (s32[128]{0:T(128)}, s32[128]{0:T(128)S(1)}, u32[]{:S(2)}) copy-start(s32[128]{0:T(128)S(1)} %get-tuple-element.9) | copy-start | bytes 1540
  9.0 17.7 %collective-permute-start = (f32[32,128]{0,1:T(8,128)S(1)}, f32[32,128]{0,1:T(8,128)S(1)}, u32[]{:S(2)}, u32[]{:S(2)}) collective-permute-start(f32[32,128]{0,1:T(8,128)S(1)} %convolution_bitcast_fusion.7), channel_id=1, source_target_pairs={{0,1},{1,0},{2,3},{3,2},{4,5},{5,4},{6,7},{7,6},{8,9},{9,8},{10,11... | collective-permute-start | bytes 49160 | tf_op jit(solution)/shard_map/ppermute | solution.py:19
  13.1 15.3 %collective-permute-start.1 = (f32[32,128]{0,1:T(8,128)S(1)}, f32[32,128]{0,1:T(8,128)S(1)}, u32[]{:S(2)}, u32[]{:S(2)}) collective-permute-start(f32[32,128]{0,1:T(8,128)S(1)} %convolution_bitcast_fusion.6), channel_id=1, source_target_pairs={{0,2},{1,3},{2,0},{3,1},{4,6},{5,7},{6,4},{7,5},{8,10},{9,11},{10,... | collective-permute-start | bytes 49160 | tf_op jit(solution)/shard_map/ppermute | solution.py:19
  16.7 13.3 %collective-permute-start.2 = (f32[32,128]{0,1:T(8,128)S(1)}, f32[32,128]{0,1:T(8,128)S(1)}, u32[]{:S(2)}, u32[]{:S(2)}) collective-permute-start(f32[32,128]{0,1:T(8,128)S(1)} %convolution_bitcast_fusion.5), channel_id=1, source_target_pairs={{0,4},{1,5},{2,6},{3,7},{4,0},{5,1},{6,2},{7,3},{8,12},{9,13},{10,... | collective-permute-start | bytes 49160 | tf_op jit(solution)/shard_map/ppermute | solution.py:19
  17.7 19.6 %copy-start.1 = (f32[1,512,512]{2,1,0:T(8,128)S(1)}, f32[1,512,512]{2,1,0:T(8,128)}, u32[]{:S(2)}) copy-start(f32[1,512,512]{2,1,0:T(8,128)} %param.16) | copy-start | bytes 3145732
  17.7 13.8 %collective-permute-start.3 = (f32[32,128]{0,1:T(8,128)S(1)}, f32[32,128]{0,1:T(8,128)S(1)}, u32[]{:S(2)}, u32[]{:S(2)}) collective-permute-start(f32[32,128]{0,1:T(8,128)S(1)} %convolution_bitcast_fusion.4), channel_id=1, source_target_pairs={{0,8},{1,9},{2,10},{3,11},{4,12},{5,13},{6,14},{7,15},{8,0},{9,1},... | collective-permute-start | bytes 49160 | tf_op jit(solution)/shard_map/ppermute | solution.py:19
  33.8 20.4 %copy-start.5 = (f32[32,2048]{1,0:T(8,128)}, f32[32,2048]{1,0:T(8,128)S(1)}, u32[]{:S(2)}) copy-start(f32[32,2048]{1,0:T(8,128)S(1)} %get-tuple-element.23) | copy-start | bytes 786436
  33.8 33.7 %copy-start.7 = (f32[12,128,128]{2,1,0:T(8,128)S(1)}, f32[12,128,128]{2,1,0:T(8,128)}, u32[]{:S(2)}) copy-start(f32[12,128,128]{2,1,0:T(8,128)} %param.15) | copy-start | bytes 2359300
  36.7 133.4 %reduce-scatter.5.cloned.1.call-start = ((), (), s32[]{:S(2)}) async-start(), calls=%async_computation.3 | async-start | bytes 163840 | tf_op jit(solution)/shard_map/reduce_scatter | solution.py:78
  37.3 35.9 %copy-start.22 = (s32[1,4]{1,0:T(1,128)S(1)}, s32[1,4]{1,0:T(1,128)}, u32[]{:S(2)}) copy-start(s32[1,4]{1,0:T(1,128)} %param.21) | copy-start | bytes 52
  55.7 5.8 %collective-permute-start.4 = (f32[8,1024]{1,0:T(8,128)S(1)}, f32[8,1024]{1,0:T(8,128)S(1)}, u32[]{:S(2)}, u32[]{:S(2)}) collective-permute-start(f32[8,1024]{1,0:T(8,128)S(1)} %reshape.579), channel_id=1, source_target_pairs={{0,1},{1,2},{2,3},{3,0},{4,5},{5,6},{6,7},{7,4},{8,9},{9,10},{10,1... | collective-permute-start | bytes 98312 | tf_op jit(solution)/shard_map/ppermute | solution.py:84
  61.5 6.0 %collective-permute-start.5 = (f32[8,1024]{1,0:T(8,128)S(1)}, f32[8,1024]{1,0:T(8,128)S(1)}, u32[]{:S(2)}, u32[]{:S(2)}) collective-permute-start(f32[8,1024]{1,0:T(8,128)S(1)} %collective-permute-done.4), channel_id=1, source_target_pairs={{0,1},{1,2},{2,3},{3,0},{4,5},{5,6},{6,7},{7,4},{8,9},{9,10},{10,1... | collective-permute-start | bytes 98312 | tf_op jit(solution)/shard_map/ppermute | solution.py:84
  67.5 5.7 %collective-permute-start.6 = (f32[8,1024]{1,0:T(8,128)S(1)}, f32[8,1024]{1,0:T(8,128)S(1)}, u32[]{:S(2)}, u32[]{:S(2)}) collective-permute-start(f32[8,1024]{1,0:T(8,128)S(1)} %collective-permute-done.5), channel_id=1, source_target_pairs={{0,1},{1,2},{2,3},{3,0},{4,5},{5,6},{6,7},{7,4},{8,9},{9,10},{10,1... | collective-permute-start | bytes 98312 | tf_op jit(solution)/shard_map/ppermute | solution.py:84
  75.7 3.7 %collective-permute-start.7 = (f32[32,128]{1,0:T(8,128)S(1)}, f32[32,128]{1,0:T(8,128)S(1)}, u32[]{:S(2)}, u32[]{:S(2)}) collective-permute-start(f32[32,128]{1,0:T(8,128)S(1)} %fusion.73), channel_id=1, source_target_pairs={{0,1},{1,0},{2,3},{3,2},{4,5},{5,4},{6,7},{7,6},{8,9},{9,8},{10,11... | collective-permute-start | bytes 49160 | tf_op jit(solution)/shard_map/ppermute | solution.py:19
  75.9 4.7 %collective-permute-start.8 = (f32[32,128]{1,0:T(8,128)S(1)}, f32[32,128]{1,0:T(8,128)S(1)}, u32[]{:S(2)}, u32[]{:S(2)}) collective-permute-start(f32[32,128]{1,0:T(8,128)S(1)} %fusion.69), channel_id=1, source_target_pairs={{0,2},{1,3},{2,0},{3,1},{4,6},{5,7},{6,4},{7,5},{8,10},{9,11},{10,... | collective-permute-start | bytes 49160 | tf_op jit(solution)/shard_map/ppermute | solution.py:19
  76.3 5.2 %collective-permute-start.9 = (f32[32,128]{1,0:T(8,128)S(1)}, f32[32,128]{1,0:T(8,128)S(1)}, u32[]{:S(2)}, u32[]{:S(2)}) collective-permute-start(f32[32,128]{1,0:T(8,128)S(1)} %fusion.65), channel_id=1, source_target_pairs={{0,4},{1,5},{2,6},{3,7},{4,0},{5,1},{6,2},{7,3},{8,12},{9,13},{10,... | collective-permute-start | bytes 49160 | tf_op jit(solution)/shard_map/ppermute | solution.py:19
  76.3 6.0 %collective-permute-start.10 = (f32[32,128]{1,0:T(8,128)S(1)}, f32[32,128]{1,0:T(8,128)S(1)}, u32[]{:S(2)}, u32[]{:S(2)}) collective-permute-start(f32[32,128]{1,0:T(8,128)S(1)} %fusion.61), channel_id=1, source_target_pairs={{0,8},{1,9},{2,10},{3,11},{4,12},{5,13},{6,14},{7,15},{8,0},{9,1},... | collective-permute-start | bytes 49160 | tf_op jit(solution)/shard_map/ppermute | solution.py:19
  84.0 17.5 %copy-start.12 = (f32[32,128]{1,0:T(8,128)S(1)}, f32[32,128]{1,0:T(8,128)}, u32[]{:S(2)}) copy-start(f32[32,128]{1,0:T(8,128)} %get-tuple-element.24) | copy-start | bytes 49156
  93.9 12.4 %copy-start.6 = (f32[32,2048]{1,0:T(8,128)S(1)}, f32[32,2048]{1,0:T(8,128)}, u32[]{:S(2)}) copy-start(f32[32,2048]{1,0:T(8,128)} %copy-done.5) | copy-start | bytes 786436
  95.7 6.4 %collective-permute-start.11 = (f32[32,128]{1,0:T(8,128)S(1)}, f32[32,128]{1,0:T(8,128)S(1)}, u32[]{:S(2)}, u32[]{:S(2)}) collective-permute-start(f32[32,128]{1,0:T(8,128)S(1)} %fusion.72), channel_id=1, source_target_pairs={{0,1},{1,0},{2,3},{3,2},{4,5},{5,4},{6,7},{7,6},{8,9},{9,8},{10,11... | collective-permute-start | bytes 49160 | tf_op jit(solution)/shard_map/ppermute | solution.py:19
  97.7 5.3 %collective-permute-start.12 = (f32[32,128]{1,0:T(8,128)S(1)}, f32[32,128]{1,0:T(8,128)S(1)}, u32[]{:S(2)}, u32[]{:S(2)}) collective-permute-start(f32[32,128]{1,0:T(8,128)S(1)} %fusion.68), channel_id=1, source_target_pairs={{0,2},{1,3},{2,0},{3,1},{4,6},{5,7},{6,4},{7,5},{8,10},{9,11},{10,... | collective-permute-start | bytes 49160 | tf_op jit(solution)/shard_map/ppermute | solution.py:19
  98.5 6.1 %collective-permute-start.13 = (f32[32,128]{1,0:T(8,128)S(1)}, f32[32,128]{1,0:T(8,128)S(1)}, u32[]{:S(2)}, u32[]{:S(2)}) collective-permute-start(f32[32,128]{1,0:T(8,128)S(1)} %fusion.64), channel_id=1, source_target_pairs={{0,4},{1,5},{2,6},{3,7},{4,0},{5,1},{6,2},{7,3},{8,12},{9,13},{10,... | collective-permute-start | bytes 49160 | tf_op jit(solution)/shard_map/ppermute | solution.py:19
  98.5 6.9 %collective-permute-start.14 = (f32[32,128]{1,0:T(8,128)S(1)}, f32[32,128]{1,0:T(8,128)S(1)}, u32[]{:S(2)}, u32[]{:S(2)}) collective-permute-start(f32[32,128]{1,0:T(8,128)S(1)} %fusion.60), channel_id=1, source_target_pairs={{0,8},{1,9},{2,10},{3,11},{4,12},{5,13},{6,14},{7,15},{8,0},{9,1},... | collective-permute-start | bytes 49160 | tf_op jit(solution)/shard_map/ppermute | solution.py:19
  103.0 49.1 %copy-start.2 = (f32[1,512,512]{2,1,0:T(8,128)S(1)}, f32[1,512,512]{2,1,0:T(8,128)}, u32[]{:S(2)}) copy-start(f32[1,512,512]{2,1,0:T(8,128)} %param.16) | copy-start | bytes 3145732
  147.3 37.1 %copy-start.8 = (f32[12,128,128]{2,1,0:T(8,128)S(1)}, f32[12,128,128]{2,1,0:T(8,128)}, u32[]{:S(2)}) copy-start(f32[12,128,128]{2,1,0:T(8,128)} %param.15) | copy-start | bytes 2359300
  152.1 38.0 %copy-start.23 = (s32[1,4]{1,0:T(1,128)S(1)}, s32[1,4]{1,0:T(1,128)}, u32[]{:S(2)}) copy-start(s32[1,4]{1,0:T(1,128)} %param.21) | copy-start | bytes 52
  172.5 5.8 %collective-permute-start.15 = (f32[8,1024]{1,0:T(8,128)S(1)}, f32[8,1024]{1,0:T(8,128)S(1)}, u32[]{:S(2)}, u32[]{:S(2)}) collective-permute-start(f32[8,1024]{1,0:T(8,128)S(1)} %reshape.587), channel_id=1, source_target_pairs={{0,1},{1,2},{2,3},{3,0},{4,5},{5,6},{6,7},{7,4},{8,9},{9,10},{10,1... | collective-permute-start | bytes 98312 | tf_op jit(solution)/shard_map/ppermute | solution.py:84
  178.3 6.1 %collective-permute-start.16 = (f32[8,1024]{1,0:T(8,128)S(1)}, f32[8,1024]{1,0:T(8,128)S(1)}, u32[]{:S(2)}, u32[]{:S(2)}) collective-permute-start(f32[8,1024]{1,0:T(8,128)S(1)} %collective-permute-done.15), channel_id=1, source_target_pairs={{0,1},{1,2},{2,3},{3,0},{4,5},{5,6},{6,7},{7,4},{8,9},{9,10},{10,1... | collective-permute-start | bytes 98312 | tf_op jit(solution)/shard_map/ppermute | solution.py:84
  184.3 5.7 %collective-permute-start.17 = (f32[8,1024]{1,0:T(8,128)S(1)}, f32[8,1024]{1,0:T(8,128)S(1)}, u32[]{:S(2)}, u32[]{:S(2)}) collective-permute-start(f32[8,1024]{1,0:T(8,128)S(1)} %collective-permute-done.16), channel_id=1, source_target_pairs={{0,1},{1,2},{2,3},{3,0},{4,5},{5,6},{6,7},{7,4},{8,9},{9,10},{10,1... | collective-permute-start | bytes 98312 | tf_op jit(solution)/shard_map/ppermute | solution.py:84
  190.3 50.4 %copy-start.27 = (f32[32]{0:T(128)S(1)}, f32[32]{0:T(128)}, u32[]{:S(2)}) copy-start(f32[32]{0:T(128)} %copy-done.26) | copy-start | bytes 388
  191.8 3.8 %collective-permute-start.18 = (f32[32,128]{1,0:T(8,128)S(1)}, f32[32,128]{1,0:T(8,128)S(1)}, u32[]{:S(2)}, u32[]{:S(2)}) collective-permute-start(f32[32,128]{1,0:T(8,128)S(1)} %fusion.71), channel_id=1, source_target_pairs={{0,1},{1,0},{2,3},{3,2},{4,5},{5,4},{6,7},{7,6},{8,9},{9,8},{10,11... | collective-permute-start | bytes 49160 | tf_op jit(solution)/shard_map/ppermute | solution.py:19
  192.1 4.7 %collective-permute-start.19 = (f32[32,128]{1,0:T(8,128)S(1)}, f32[32,128]{1,0:T(8,128)S(1)}, u32[]{:S(2)}, u32[]{:S(2)}) collective-permute-start(f32[32,128]{1,0:T(8,128)S(1)} %fusion.67), channel_id=1, source_target_pairs={{0,2},{1,3},{2,0},{3,1},{4,6},{5,7},{6,4},{7,5},{8,10},{9,11},{10,... | collective-permute-start | bytes 49160 | tf_op jit(solution)/shard_map/ppermute | solution.py:19
  192.4 5.2 %collective-permute-start.20 = (f32[32,128]{1,0:T(8,128)S(1)}, f32[32,128]{1,0:T(8,128)S(1)}, u32[]{:S(2)}, u32[]{:S(2)}) collective-permute-start(f32[32,128]{1,0:T(8,128)S(1)} %fusion.63), channel_id=1, source_target_pairs={{0,4},{1,5},{2,6},{3,7},{4,0},{5,1},{6,2},{7,3},{8,12},{9,13},{10,... | collective-permute-start | bytes 49160 | tf_op jit(solution)/shard_map/ppermute | solution.py:19
  192.4 6.0 %collective-permute-start.21 = (f32[32,128]{1,0:T(8,128)S(1)}, f32[32,128]{1,0:T(8,128)S(1)}, u32[]{:S(2)}, u32[]{:S(2)}) collective-permute-start(f32[32,128]{1,0:T(8,128)S(1)} %fusion.59), channel_id=1, source_target_pairs={{0,8},{1,9},{2,10},{3,11},{4,12},{5,13},{6,14},{7,15},{8,0},{9,1},... | collective-permute-start | bytes 49160 | tf_op jit(solution)/shard_map/ppermute | solution.py:19
  199.3 41.4 %copy-start.3 = (f32[32,2048]{1,0:T(8,128)}, f32[32,2048]{1,0:T(8,128)S(1)}, u32[]{:S(2)}) copy-start(f32[32,2048]{1,0:T(8,128)S(1)} %get-tuple-element.47) | copy-start | bytes 786436
  251.5 49.8 %copy-start.29 = (f32[32]{0:T(128)S(1)}, f32[32]{0:T(128)}, u32[]{:S(2)}) copy-start(f32[32]{0:T(128)} %copy-done.28) | copy-start | bytes 388
  251.5 49.8 %copy-start.9 = (f32[1,32,2048]{2,1,0:T(8,128)S(1)}, f32[1,32,2048]{2,1,0:T(8,128)}, u32[]{:S(2)}) copy-start(f32[1,32,2048]{2,1,0:T(8,128)} %get-tuple-element.58) | copy-start | bytes 786436
  251.5 49.8 %copy-start.10 = (f32[1,32,2048]{2,1,0:T(8,128)S(1)}, f32[1,32,2048]{2,1,0:T(8,128)}, u32[]{:S(2)}) copy-start(f32[1,32,2048]{2,1,0:T(8,128)} %constant_dynamic-update-slice_fusion.33) | copy-start | bytes 786436
  251.5 49.8 %copy-start.11 = (f32[1,32,2048]{2,1,0:T(8,128)S(1)}, f32[1,32,2048]{2,1,0:T(8,128)}, u32[]{:S(2)}) copy-start(f32[1,32,2048]{2,1,0:T(8,128)} %get-tuple-element.57) | copy-start | bytes 786436
  251.5 49.8 %copy-start.25 = (f32[32]{0:T(128)S(1)}, f32[32]{0:T(128)}, u32[]{:S(2)}) copy-start(f32[32]{0:T(128)} %copy-done.24) | copy-start | bytes 388
  252.6 6.4 %collective-permute-start.22 = (f32[32,128]{1,0:T(8,128)S(1)}, f32[32,128]{1,0:T(8,128)S(1)}, u32[]{:S(2)}, u32[]{:S(2)}) collective-permute-start(f32[32,128]{1,0:T(8,128)S(1)} %fusion.70), channel_id=1, source_target_pairs={{0,1},{1,0},{2,3},{3,2},{4,5},{5,4},{6,7},{7,6},{8,9},{9,8},{10,11... | collective-permute-start | bytes 49160 | tf_op jit(solution)/shard_map/ppermute | solution.py:19
  252.7 7.2 %collective-permute-start.23 = (f32[32,128]{1,0:T(8,128)S(1)}, f32[32,128]{1,0:T(8,128)S(1)}, u32[]{:S(2)}, u32[]{:S(2)}) collective-permute-start(f32[32,128]{1,0:T(8,128)S(1)} %fusion.66), channel_id=1, source_target_pairs={{0,2},{1,3},{2,0},{3,1},{4,6},{5,7},{6,4},{7,5},{8,10},{9,11},{10,... | collective-permute-start | bytes 49160 | tf_op jit(solution)/shard_map/ppermute | solution.py:19
  254.8 5.9 %collective-permute-start.24 = (f32[32,128]{1,0:T(8,128)S(1)}, f32[32,128]{1,0:T(8,128)S(1)}, u32[]{:S(2)}, u32[]{:S(2)}) collective-permute-start(f32[32,128]{1,0:T(8,128)S(1)} %fusion.62), channel_id=1, source_target_pairs={{0,4},{1,5},{2,6},{3,7},{4,0},{5,1},{6,2},{7,3},{8,12},{9,13},{10,... | collective-permute-start | bytes 49160 | tf_op jit(solution)/shard_map/ppermute | solution.py:19
  254.8 6.7 %collective-permute-start.25 = (f32[32,128]{1,0:T(8,128)S(1)}, f32[32,128]{1,0:T(8,128)S(1)}, u32[]{:S(2)}, u32[]{:S(2)}) collective-permute-start(f32[32,128]{1,0:T(8,128)S(1)} %fusion.58), channel_id=1, source_target_pairs={{0,8},{1,9},{2,10},{3,11},{4,12},{5,13},{6,14},{7,15},{8,0},{9,1},... | collective-permute-start | bytes 49160 | tf_op jit(solution)/shard_map/ppermute | solution.py:19
  (10 other events, 46.9 us)
Sparse Core Ops, SparseCore 0:
  36.8 16.4 reduce-scatter.2
  150.3 19.8 reduce-scatter.4
